TPU v7x, 256 devices: a whole 4x4x8 slice. The times are simulated.
256 devices in a mesh: hyp: 4 (over z_lo), row: 16 (over x, z_hi, core), col: 4 (over y).
Axes of the slice: x: 4, y: 4, z: 8 (z_hi: 2, z_lo: 4; z = z_hi * 4 + z_lo), core: 2. Of those that a mesh axis runs over, the one named last changes fastest.
Arguments:
- front_orig: bfloat16 [40960, 10240], P(('hyp', 'row'), 'col'), parts along dimension 0, as said below
- child_updates: bfloat16 [65536, 8192], P(('hyp', 'row'), 'col'), parts along dimension 0, as said below
- child_map: int32 [8, 64], P('hyp'), parts along dimension 0, may hold values from 0 to 79, as said below
- panel_inverse: bfloat16 [1024, 256], P('hyp'), parts along dimension 0, as said below
Outputs:
- schur: bfloat16 [40960, 10240], P(('hyp', 'row'), 'col'), parts along dimension 0
- panel: bfloat16 [40960, 256], P(('hyp', 'row')), parts along dimension 0
There are 4 independent parts, one for each index of `hyp`. A program takes and returns all parts, laid end to end along the dimension named above; each array names one. Nothing has to cross between parts.
Inputs may be any that keep to these rules, and one draw needn't show every extreme that they name: `child_map`: each child's entries are distinct. Parent block p lies on row index p // 5 and column index p // 20. Of the 8 blocks of a child on one row index (child c on row indices c * 8 to (c + 1) * 8 - 1, in order), at most 1 lie on one parent row index; of the 16 blocks on one column index, at most 4 lie on one parent column index. Every parent row index receives the same number of blocks of each child. `child_updates`: each child's update block is symmetric. `front_orig`: Symmetric. `panel_inverse`: upper triangular with a positive diagonal.
All inputs are finite; a program needn't handle non-finite values.
Results may differ from a plain program's by a relative error of at most 0.0052.
Values may be sent and summed in bfloat16 or wider, within the bound.
No kernel may reach another device: no remote copies, remote signals or barrier semaphores. Data moves between devices by JAX's collectives and lax.ppermute only.
A program may use at most 128 MiB of HBM per device.

v0:
```python
import jax
import jax.numpy as jnp
from jax import lax
from jax.sharding import PartitionSpec as P

B = 128
PANEL = 256


def picked(shard, axis, root):
    return lax.dynamic_index_in_dim(lax.all_gather(shard, axis), root, 0, keepdims=False)


def one_hot(indices, columns):
    return (indices[..., None] == jnp.arange(columns, dtype=jnp.int32)).astype(jnp.bfloat16)


def earlier_same(labels):
    length = labels.shape[-1]
    matches = labels[..., :, None] == labels[..., None, :]
    before = jnp.arange(length)[None, :] < jnp.arange(length)[:, None]
    return jnp.sum(matches & before, axis=-1)


def send_table(block_ids, owner_width, capacity, owners_count):
    owners = block_ids // owner_width
    slots = owners * capacity + earlier_same(owners)
    return one_hot(slots, owners_count * capacity)


def receive_table(all_ids, owner_width, my_index, capacity):
    owners = all_ids // owner_width
    rank_in = earlier_same(owners)
    local_block = all_ids - my_index * owner_width
    arrives = (owners == my_index)[:, :, None, None]
    slot_match = rank_in[:, :, None, None] == jnp.arange(capacity)[None, None, :, None]
    block_match = local_block[:, :, None, None] == jnp.arange(owner_width)[None, None, None, :]
    table = jnp.sum(arrives & slot_match & block_match, axis=1)
    return table.reshape(-1, owner_width).astype(jnp.bfloat16)


def local(front_orig, child_updates, child_map, panel_inverse):
    n_row = lax.axis_size("row")
    n_col = lax.axis_size("col")
    me_row = lax.axis_index("row")
    me_col = lax.axis_index("col")
    rows_local, cols_local = child_updates.shape
    part_rows, part_cols = front_orig.shape
    senders = n_row // 2
    child_index = me_row // senders
    blocks_row = rows_local // B
    blocks_col = cols_local // B
    fine_count = max(n_row, n_col)
    parent_row_blocks = part_rows // B
    parent_col_blocks = part_cols // B
    row_cap = max(1, blocks_row // fine_count) * (fine_count // n_row)
    col_cap = max(1, blocks_col // fine_count) * (fine_count // n_col)
    my_map = lax.dynamic_index_in_dim(child_map, child_index, 0, keepdims=False)
    flat_map = child_map.reshape(-1)
    row_ids = lax.dynamic_slice_in_dim(flat_map, me_row * blocks_row, blocks_row)
    row_send = send_table(row_ids, parent_row_blocks, row_cap, n_row)
    row_receive = receive_table(
        child_map.reshape(n_row, blocks_row), parent_row_blocks, me_row, row_cap
    )
    col_ids = lax.dynamic_slice_in_dim(my_map, me_col * blocks_col, blocks_col)
    col_send = send_table(col_ids, parent_col_blocks, col_cap, n_col).reshape(
        blocks_col, n_col, col_cap
    )
    row_pick = row_send.reshape(blocks_row, n_row, row_cap)
    tiles_four = child_updates.reshape(blocks_row, B, blocks_col, B)
    outgoing = jnp.einsum(
        "ibjc,ipa,jqe->pqabec", tiles_four, row_pick, col_send, preferred_element_type=jnp.float32
    ).astype(jnp.bfloat16)
    outgoing = outgoing.reshape(n_row * n_col, row_cap * B, col_cap * B)
    incoming = lax.all_to_all(outgoing, ("row", "col"), split_axis=0, concat_axis=0, tiled=True)
    tiles = incoming.reshape(n_row, n_col, row_cap, B, col_cap, B)
    col_tables = jnp.stack(
        [
            receive_table(
                child_map[k].reshape(n_col, blocks_col), parent_col_blocks, me_col, col_cap
            ).reshape(n_col, col_cap, parent_col_blocks)
            for k in range(2)
        ]
    )
    per_source = jnp.repeat(col_tables, senders, axis=0)
    placed_cols = jnp.einsum(
        "rsabec,rseq->rabqc", tiles, per_source, preferred_element_type=jnp.float32
    ).astype(jnp.bfloat16)
    row_table = row_receive.reshape(n_row, row_cap, parent_row_blocks)
    assembled = jnp.einsum(
        "rabqc,rap->pbqc", placed_cols, row_table, preferred_element_type=jnp.float32
    )
    front32 = assembled.reshape(part_rows, part_cols) + front_orig.astype(jnp.float32)
    front = front32.astype(jnp.bfloat16)
    local_panel = jnp.dot(
        front[:, :PANEL], panel_inverse, preferred_element_type=jnp.float32
    ).astype(jnp.bfloat16)
    row_panel = picked(local_panel, "col", 0)
    all_panel = lax.all_gather(row_panel, "row", axis=0, tiled=True)
    col_panel = lax.dynamic_slice_in_dim(all_panel, me_col * part_cols, part_cols, 0)
    update = lax.dot_general(
        row_panel, col_panel, (((1,), (1,)), ((), ())), preferred_element_type=jnp.float32
    )
    schur = (front.astype(jnp.float32) - update).astype(jnp.bfloat16)
    return (schur, row_panel)


def solution(mesh):
    in_specs = (P(("hyp", "row"), "col"), P(("hyp", "row"), "col"), P("hyp", None), P("hyp", None))
    out_specs = (P(("hyp", "row"), "col"), P(("hyp", "row"), None))
    return jax.shard_map(local, mesh=mesh, in_specs=in_specs, out_specs=out_specs, check_vma=False)
```

profile of v0, /device:TPU:1, one launch (start us, length us, event | category | flops | bytes accessed | tf_op | source)
XLA Modules:
  0.0 411.4 jit_solution(8262552116973549749)
XLA Ops:
  7.2 0.0 copy-start
  7.2 0.8 reshape.440
  8.0 0.1 and_select_fusion
  8.1 0.2 convert_reduce_fusion.7
  8.3 0.1 fusion.30
  8.4 0.8 bitcast_select_fusion
  9.2 0.2 convert_reduce_fusion.6
  9.3 3.6 copy.26
  12.9 1.3 fusion.13
  14.3 8.8 %convert_bitcast_fusion = bf16[16,4,1,128,4,128]{5,0,3,4,1,2:T(8,128)(2,1)} fusion(bf16[4,4,8,128,128]{4,1,3,2,0:T(4,128)(2,1)S(1)} %fusion.13, s32[8]{0:T(128)S(1)} %fusion.30), kind=kOutput, calls=%fused_computation.6 | convolution fusion | flops 67108992 | bytes 12582944 | tf_op jit(solution)/shard_map/ibjc,ipa,jqe->pqabec/dot_general | solution.py:71
  23.1 13.7 %copy.17 = bf16[16,4,1,128,4,128]{3,5,4,1,0,2:T(8,128)(2,1)} copy(bf16[16,4,1,128,4,128]{5,0,3,4,1,2:T(8,128)(2,1)} %convert_bitcast_fusion) | data formatting | bytes 16777216 | tf_op jit(solution)/shard_map/convert_element_type | solution.py:73
  36.8 0.0 copy-start.1
  36.8 15.9 %all-to-all-start = ((bf16[64,128,512]{1,2,0:T(8,128)(2,1)}), bf16[64,128,512]{1,2,0:T(8,128)(2,1)}, u32[]{:S(2)}, u32[]{:S(2)}) async-start(bf16[64,128,512]{1,2,0:T(8,128)(2,1)} %bitcast.62), calls=%async_computation | async-start | bytes 16777216 | tf_op jit(solution)/shard_map/all_to_all | solution.py:75
  52.7 0.2 all-gather.6.cloned.1.call-start
  53.0 0.0 copy-done.1
  53.0 0.1 and.196
  53.1 0.1 and.205
  53.2 0.1 and.189
  53.3 0.1 copy.12
  53.4 0.1 div.95
  53.5 0.1 div.97
  53.6 0.1 sub.77
  53.7 0.1 sub.80
  53.8 0.3 convert_reduce_fusion.3
  54.1 0.1 iota_compare_fusion
  54.2 0.1 convert_reduce_fusion
  54.3 0.1 iota_compare_fusion.1
  54.4 0.1 convert_reduce_fusion.1
  54.6 0.1 div.93
  54.7 0.1 copy.11
  54.7 0.1 sub.73
  54.8 0.1 copy.14
  54.9 0.1 convert_reduce_fusion.4
  55.0 183.0 %all-to-all-done = bf16[64,128,512]{1,2,0:T(8,128)(2,1)} async-done(((bf16[64,128,512]{1,2,0:T(8,128)(2,1)}), bf16[64,128,512]{1,2,0:T(8,128)(2,1)}, u32[]{:S(2)}, u32[]{:S(2)}) %all-to-all-start) | async-done | bytes 8388640 | tf_op jit(solution)/shard_map/all_to_all | solution.py:75
  238.0 14.6 %copy.18 = bf16[16,4,128,4,128]{4,1,3,2,0:T(4,128)(2,1)} copy(bf16[16,4,128,4,128]{2,4,3,1,0:T(8,128)(2,1)} %bitcast.17) | data formatting | bytes 16777216 | tf_op jit(solution)/shard_map/reshape.31
  252.6 12.2 %fusion = bf16[16,128,20,128]{3,2,1,0:T(8,128)(2,1)} fusion(bf16[16,4,4,20,1]{3,1,2,4,0:T(4,128)(2,1)S(1)} %bitcast.66, bf16[16,4,128,4,128]{4,1,3,2,0:T(4,128)(2,1)} %copy.18), kind=kOutput, calls=%fused_computation.1 | convolution fusion | flops 173015040 | bytes 18884608 | tf_op jit(solution)/shard_map/rsabec,rseq->rabqc/dot_general | solution.py:86
  264.8 11.1 %fusion.1 = f32[5,128,20,128]{3,0,2,1:T(8,128)S(1)} fusion(bf16[16,128,20,128]{3,2,1,0:T(8,128)(2,1)} %fusion, s32[16,5]{0,1:T(8,128)S(1)} %convert_reduce_fusion.5), kind=kOutput, calls=%fused_computation.2 | convolution fusion | flops 52428880 | bytes 17039680 | tf_op jit(solution)/shard_map/rabqc,rap->pbqc/dot_general | solution.py:90
  275.9 1.3 copy.20
  277.3 3.5 fusion.7
  280.8 0.0 copy-done
  280.8 1.0 convolution_convert_fusion
  281.8 0.0 all-gather.6.cloned.1.call-update
  281.8 0.0 all-gather.8.cloned.1.call-start
  281.8 28.4 %all-gather.6.cloned.1.call-done = bf16[2560,256]{1,0:T(8,128)(2,1)} async-done(((bf16[640,256]{1,0:T(8,128)(2,1)}), bf16[2560,256]{1,0:T(8,128)(2,1)}) %all-gather.6.cloned.1.call-update) | async-done | bytes 1310736 | tf_op jit(solution)/shard_map/all_gather | solution.py:11
  310.2 1.7 slice.15
  311.9 0.0 all-gather.8.cloned.1.call-update
  312.0 88.4 %all-gather.8.cloned.1.call-done = bf16[10240,256]{1,0:T(8,128)(2,1)} async-done(((bf16[640,256]{1,0:T(8,128)(2,1)}), bf16[10240,256]{1,0:T(8,128)(2,1)}) %all-gather.8.cloned.1.call-update) | async-done | bytes 5242896 | tf_op jit(solution)/shard_map/all_gather | solution.py:99
  400.3 4.2 %subtract_convert_fusion = bf16[640,2560]{1,0:T(8,128)(2,1)} fusion(bf16[640,2560]{1,0:T(8,128)(2,1)S(1)} %fusion.7, bf16[640,256]{1,0:T(8,128)(2,1)} %slice.15, bf16[10240,256]{1,0:T(8,128)(2,1)} %all-gather.8.cloned.1.call-done, s32[]{:T(128)S(6)} %select_n.105), kind=kOutput, calls=%fused_computation.9 | convolution fusion | flops 843776000 | bytes 8192004 | tf_op jit(solution)/shard_map/dot_general | solution.py:101
  (20 shorter events, 0.2 us)
Async XLA Ops:
  7.2 273.6 %copy-start = (bf16[256,256]{1,0:T(8,128)(2,1)S(1)}, bf16[256,256]{1,0:T(8,128)(2,1)}, u32[]{:S(2)}) copy-start(bf16[256,256]{1,0:T(8,128)(2,1)} %param.7) | copy-start | bytes 393220
  36.8 16.2 %copy-start.1 = (s32[2,64]{1,0:T(2,128)S(1)}, s32[2,64]{1,0:T(2,128)}, u32[]{:S(2)}) copy-start(s32[2,64]{1,0:T(2,128)} %param.6) | copy-start | bytes 1540
  36.8 201.2 %all-to-all-start = ((bf16[64,128,512]{1,2,0:T(8,128)(2,1)}), bf16[64,128,512]{1,2,0:T(8,128)(2,1)}, u32[]{:S(2)}, u32[]{:S(2)}) async-start(bf16[64,128,512]{1,2,0:T(8,128)(2,1)} %bitcast.62), calls=%async_computation | async-start | bytes 16777216 | tf_op jit(solution)/shard_map/all_to_all | solution.py:75
  52.7 257.5 %all-gather.6.cloned.1.call-start = ((), (), s32[]{:S(2)}) async-start(), calls=%async_computation.1 | async-start | bytes 1638400 | tf_op jit(solution)/shard_map/all_gather | solution.py:11
  281.8 118.6 %all-gather.8.cloned.1.call-start = ((), (), s32[]{:S(2)}) async-start(), calls=%async_computation.2 | async-start | bytes 5570560 | tf_op jit(solution)/shard_map/all_gather | solution.py:99
Sparse Core Ops, SparseCore 0:
  281.9 28.2 all-gather.5
  313.5 86.8 all-gather.7
where the time goes:
time: 412 us; the launch traced here: 411 us
  waiting for transfers between devices  300 us (73%)
  matrix products  38.6 us (9%)
  local copies, waits for them, and re-layouts  36.8 us (9%)
  starting transfers between devices  16.2 us (4%)
  between operations  14.3 us (3%)
  other arithmetic  5.78 us (1%)
    all_to_all x1, waiting for transfers between devices, local(): lax.all_to_all(outgoing, ('row', 'col'), split_axis=0, concat_axis=0, til...  183 us
    all_gather x1, waiting for transfers between devices, local(): all_panel = lax.all_gather(row_panel, 'row', axis=0, tiled=True)  88.4 us
    all_gather x1, waiting for transfers between devices, picked(): lax.all_gather(shard, axis)  28.4 us
    all_to_all x1, starting transfers between devices, local(): lax.all_to_all(outgoing, ('row', 'col'), split_axis=0, concat_axis=0, til...  15.9 us
    another operation x1, local copies, waits for them, and re-layouts  14.6 us
    convert_element_type x1, local copies, waits for them, and re-layouts, local(): outgoing = jnp.einsum('ibjc,ipa,jqe->pqabec', tiles_four, row_pick, col_s...  13.7 us
    dot_general x1, matrix products, local(): jnp.einsum('rsabec,rseq->rabqc', tiles, per_source, preferred_element_typ...  12.2 us
    dot_general x1, matrix products, local(): jnp.einsum('rabqc,rap->pbqc', placed_cols, row_table, preferred_element_t...  11.1 us
  transfers between devices with their start and end apart: 3, of which 3 were waited for; matrix products, arithmetic and copies ran while one was open for 0% of the time, Pallas kernels for 0%

commit v1 on v0

--- a/solution.py
+++ b/solution.py
@@ -5,6 +5,13 @@
 
 B = 128
 PANEL = 256
+
+
+def all_by_exchange(x, name, d):
+    count = lax.axis_size(name)
+    blocks = jnp.stack([x for _ in range(count)])
+    blocks = lax.all_to_all(blocks, name, split_axis=0, concat_axis=0)
+    return jnp.concatenate(blocks, axis=d)
 
 
 def picked(shard, axis, root):
@@ -96,7 +103,7 @@
         front[:, :PANEL], panel_inverse, preferred_element_type=jnp.float32
     ).astype(jnp.bfloat16)
     row_panel = picked(local_panel, "col", 0)
-    all_panel = lax.all_gather(row_panel, "row", axis=0, tiled=True)
+    all_panel = all_by_exchange(row_panel, "row", 0)
     col_panel = lax.dynamic_slice_in_dim(all_panel, me_col * part_cols, part_cols, 0)
     update = lax.dot_general(
         row_panel, col_panel, (((1,), (1,)), ((), ())), preferred_element_type=jnp.float32

time: 412 us -> 461 us (1.12)
  waiting for transfers between devices: 300 us -> 332 us
  starting transfers between devices: 16.2 us -> 27.4 us
    all_to_all x0 -> x1, waiting for transfers between devices: none -> 121 us  [all_by_exchange(): blocks = lax.all_to_all(blocks, name, split_axis=0, concat_axis=0)]
    all_gather x1 -> x0, waiting for transfers between devices: 88.4 us -> none  [local(): all_panel = lax.all_gather(row_panel, 'row', axis=0, tiled=True)]
    all_to_all x0 -> x1, starting transfers between devices: none -> 11.5 us  [all_by_exchange(): blocks = lax.all_to_all(blocks, name, split_axis=0, concat_axis=0)]
    another operation x1 -> x2, local copies, waits for them, and re-layouts: 14.6 us -> 17.4 us
where the time goes in v1:
time: 461 us; the launch traced here: 460 us
  waiting for transfers between devices  332 us (72%)
  local copies, waits for them, and re-layouts  41.3 us (9%)
  matrix products  38.6 us (8%)
  starting transfers between devices  27.4 us (6%)
  between operations  14.3 us (3%)
  other arithmetic  5.78 us (1%)
    all_to_all x1, waiting for transfers between devices, local(): lax.all_to_all(outgoing, ('row', 'col'), split_axis=0, concat_axis=0, til...  183 us
    all_to_all x1, waiting for transfers between devices, all_by_exchange(): blocks = lax.all_to_all(blocks, name, split_axis=0, concat_axis=0)  121 us
    all_gather x1, waiting for transfers between devices, picked(): lax.all_gather(shard, axis)  28.4 us
    all_to_all x1, starting transfers between devices, local(): lax.all_to_all(outgoing, ('row', 'col'), split_axis=0, concat_axis=0, til...  15.9 us
    another operation x1, local copies, waits for them, and re-layouts  14.6 us
    convert_element_type x1, local copies, waits for them, and re-layouts, local(): outgoing = jnp.einsum('ibjc,ipa,jqe->pqabec', tiles_four, row_pick, col_s...  13.7 us
    dot_general x1, matrix products, local(): jnp.einsum('rsabec,rseq->rabqc', tiles, per_source, preferred_element_typ...  12.2 us
    all_to_all x1, starting transfers between devices, all_by_exchange(): blocks = lax.all_to_all(blocks, name, split_axis=0, concat_axis=0)  11.5 us
  transfers between devices with their start and end apart: 3, of which 3 were waited for; matrix products, arithmetic and copies ran while one was open for 0% of the time, Pallas kernels for 0%

profile of v1, /device:TPU:1, one launch (start us, length us, event | category | flops | bytes accessed | tf_op | source)
XLA Modules:
  0.0 459.8 jit_solution(9858955027390113560)
XLA Ops:
  7.2 0.0 copy-start
  7.2 0.8 reshape.444
  8.0 0.1 and_select_fusion
  8.1 0.2 convert_reduce_fusion.7
  8.3 0.1 fusion.30
  8.4 0.8 bitcast_select_fusion
  9.2 0.2 convert_reduce_fusion.6
  9.3 3.6 copy.26
  12.9 1.3 fusion.13
  14.3 8.8 %convert_bitcast_fusion = bf16[16,4,1,128,4,128]{5,0,3,4,1,2:T(8,128)(2,1)} fusion(bf16[4,4,8,128,128]{4,1,3,2,0:T(4,128)(2,1)S(1)} %fusion.13, s32[8]{0:T(128)S(1)} %fusion.30), kind=kOutput, calls=%fused_computation.6 | convolution fusion | flops 67108992 | bytes 12582944 | tf_op jit(solution)/shard_map/ibjc,ipa,jqe->pqabec/dot_general | solution.py:78
  23.1 13.7 %copy.17 = bf16[16,4,1,128,4,128]{3,5,4,1,0,2:T(8,128)(2,1)} copy(bf16[16,4,1,128,4,128]{5,0,3,4,1,2:T(8,128)(2,1)} %convert_bitcast_fusion) | data formatting | bytes 16777216 | tf_op jit(solution)/shard_map/convert_element_type | solution.py:80
  36.8 15.9 %all-to-all-start = ((bf16[64,128,512]{1,2,0:T(8,128)(2,1)}), bf16[64,128,512]{1,2,0:T(8,128)(2,1)}, u32[]{:S(2)}, u32[]{:S(2)}) async-start(bf16[64,128,512]{1,2,0:T(8,128)(2,1)} %bitcast.63), calls=%async_computation | async-start | bytes 16777216 | tf_op jit(solution)/shard_map/all_to_all | solution.py:82
  52.7 0.0 all-gather.3.cloned.1.call-start
  52.8 0.1 and.196
  52.9 0.1 and.205
  53.0 0.1 and.189
  53.1 0.1 copy.12
  53.2 0.1 div.95
  53.3 0.1 div.97
  53.4 0.1 sub.77
  53.5 0.1 sub.80
  53.6 0.3 convert_reduce_fusion.3
  53.9 0.1 iota_compare_fusion
  54.0 0.1 convert_reduce_fusion
  54.1 0.1 iota_compare_fusion.1
  54.2 0.1 convert_reduce_fusion.1
  54.4 0.1 div.93
  54.5 0.1 copy.11
  54.6 0.1 sub.73
  54.6 0.1 copy.14
  54.7 0.1 convert_reduce_fusion.4
  54.9 183.1 %all-to-all-done = bf16[64,128,512]{1,2,0:T(8,128)(2,1)} async-done(((bf16[64,128,512]{1,2,0:T(8,128)(2,1)}), bf16[64,128,512]{1,2,0:T(8,128)(2,1)}, u32[]{:S(2)}, u32[]{:S(2)}) %all-to-all-start) | async-done | bytes 8388640 | tf_op jit(solution)/shard_map/all_to_all | solution.py:82
  238.0 14.6 %copy.18 = bf16[16,4,128,4,128]{4,1,3,2,0:T(4,128)(2,1)} copy(bf16[16,4,128,4,128]{2,4,3,1,0:T(8,128)(2,1)} %bitcast.17) | data formatting | bytes 16777216 | tf_op jit(solution)/shard_map/reshape.32
  252.6 12.2 %fusion = bf16[16,128,20,128]{3,2,1,0:T(8,128)(2,1)} fusion(bf16[16,4,4,20,1]{3,1,2,4,0:T(4,128)(2,1)S(1)} %bitcast.67, bf16[16,4,128,4,128]{4,1,3,2,0:T(4,128)(2,1)} %copy.18), kind=kOutput, calls=%fused_computation.1 | convolution fusion | flops 173015040 | bytes 18884608 | tf_op jit(solution)/shard_map/rsabec,rseq->rabqc/dot_general | solution.py:93
  264.8 11.1 %fusion.1 = f32[5,128,20,128]{3,0,2,1:T(8,128)S(1)} fusion(bf16[16,128,20,128]{3,2,1,0:T(8,128)(2,1)} %fusion, s32[16,5]{0,1:T(8,128)S(1)} %convert_reduce_fusion.5), kind=kOutput, calls=%fused_computation.2 | convolution fusion | flops 52428880 | bytes 17039680 | tf_op jit(solution)/shard_map/rabqc,rap->pbqc/dot_general | solution.py:97
  275.9 1.3 copy.20
  277.3 3.5 fusion.7
  280.8 0.0 copy-start.1
  280.8 1.7 copy-done.1
  282.5 1.0 convolution_convert_fusion
  283.5 0.0 all-gather.3.cloned.1.call-update
  283.5 28.4 %all-gather.3.cloned.1.call-done = bf16[2560,256]{1,0:T(8,128)(2,1)} async-done(((bf16[640,256]{1,0:T(8,128)(2,1)}), bf16[2560,256]{1,0:T(8,128)(2,1)}) %all-gather.3.cloned.1.call-update) | async-done | bytes 1310736 | tf_op jit(solution)/shard_map/all_gather | solution.py:18
  311.9 1.0 slice.15
  312.9 0.7 copy-done.3
  313.6 2.9 stack.5
  316.5 11.5 %all-to-all-start.1 = ((bf16[16,640,256]{2,1,0:T(8,128)(2,1)}), bf16[16,640,256]{2,1,0:T(8,128)(2,1)}, u32[]{:S(2)}, u32[]{:S(2)}) async-start(bf16[16,640,256]{2,1,0:T(8,128)(2,1)} %stack.5), calls=%async_computation.1 | async-start | bytes 10485760 | tf_op jit(solution)/shard_map/all_to_all | solution.py:13
  328.0 120.8 %all-to-all-done.1 = bf16[16,640,256]{2,1,0:T(8,128)(2,1)} async-done(((bf16[16,640,256]{2,1,0:T(8,128)(2,1)}), bf16[16,640,256]{2,1,0:T(8,128)(2,1)}, u32[]{:S(2)}, u32[]{:S(2)}) %all-to-all-start.1) | async-done | bytes 5242912 | tf_op jit(solution)/shard_map/all_to_all | solution.py:13
  448.8 4.2 subtract_convert_fusion
  (26 shorter events, 0.3 us)
Async XLA Ops:
  7.2 275.3 %copy-start = (bf16[256,256]{1,0:T(8,128)(2,1)S(1)}, bf16[256,256]{1,0:T(8,128)(2,1)}, u32[]{:S(2)}) copy-start(bf16[256,256]{1,0:T(8,128)(2,1)} %param.7) | copy-start | bytes 393220
  36.8 16.0 %copy-start.4 = (s32[2,64]{1,0:T(2,128)S(1)}, s32[2,64]{1,0:T(2,128)}, u32[]{:S(2)}) copy-start(s32[2,64]{1,0:T(2,128)} %param.6) | copy-start | bytes 1540
  36.8 201.2 %all-to-all-start = ((bf16[64,128,512]{1,2,0:T(8,128)(2,1)}), bf16[64,128,512]{1,2,0:T(8,128)(2,1)}, u32[]{:S(2)}, u32[]{:S(2)}) async-start(bf16[64,128,512]{1,2,0:T(8,128)(2,1)} %bitcast.63), calls=%async_computation | async-start | bytes 16777216 | tf_op jit(solution)/shard_map/all_to_all | solution.py:82
  52.7 259.2 %all-gather.3.cloned.1.call-start = ((), (), s32[]{:S(2)}) async-start(), calls=%async_computation.2 | async-start | bytes 1638400 | tf_op jit(solution)/shard_map/all_gather | solution.py:18
  280.8 1.7 copy-start.1
  312.9 0.7 copy-start.3
  316.5 132.3 %copy-start.2 = (bf16[640,2560]{1,0:T(8,128)(2,1)S(1)}, bf16[640,2560]{1,0:T(8,128)(2,1)}, u32[]{:S(2)}) copy-start(bf16[640,2560]{1,0:T(8,128)(2,1)} %copy-done.1) | copy-start | bytes 9830404
  316.5 132.3 %all-to-all-start.1 = ((bf16[16,640,256]{2,1,0:T(8,128)(2,1)}), bf16[16,640,256]{2,1,0:T(8,128)(2,1)}, u32[]{:S(2)}, u32[]{:S(2)}) async-start(bf16[16,640,256]{2,1,0:T(8,128)(2,1)} %stack.5), calls=%async_computation.1 | async-start | bytes 10485760 | tf_op jit(solution)/shard_map/all_to_all | solution.py:13
Sparse Core Ops, SparseCore 0:
  283.6 28.2 all-gather.2
